TPU v7x, 512 devices: a whole 4x4x16 slice. The times are simulated.
512 devices in a mesh: wide: 128 (over z, y, core), narrow: 4 (over x).
Axes of the slice: x: 4, y: 4, z: 16, core: 2. Of those that a mesh axis runs over, the one named last changes fastest.
Arguments:
- tokens: bfloat16 [1024, 1024], P('wide', 'narrow'), may hold values from -6 to 6
- norm_gain: float32 [1024], replicated, may hold values from 0.1 to 1.9
- w_qk: bfloat16 [1024, 2, 1024], P(None, None, 'narrow'), may hold values from -0.0625 to 0.0625
- w_value: bfloat16 [1024, 1024], P(None, 'narrow'), may hold values from -0.1875 to 0.1875
- w_out: bfloat16 [1024, 1024], P('narrow'), may hold values from -1.5 to 1.5
- kv_cache: bfloat16 [8192, 2, 32, 1024], P('wide', None, None, 'narrow'), may hold values from -200 to 200
- cache_len: int32 [1024], replicated, may hold values from 1 to 256, as said below
- page_table: int32 [1024, 8], replicated, may hold values from 0 to 63, as said below
Outputs:
- attended: bfloat16 [1024, 1024], P('wide', 'narrow')
Inputs may be any that keep to these rules, and one draw needn't show every extreme that they name: `cache_len`: every request has one or more cached positions, and some request has exactly 256. `page_table`: on every owner, the pairs (request, page) placed there by the rule of the steps occupy its 64 slots one to one.
All inputs are finite; a program needn't handle non-finite values.
Results may differ from a plain program's by a relative error of at most 0.015.
The roundings to bfloat16 on the way count: a program that leaves them out, or rounds other values in their place, can miss the bound.
Values may be sent and summed in bfloat16 or wider, within the bound.
A program may use at most 64 MiB of HBM per device.

v0:
```python
import jax
import jax.numpy as jnp
from jax import lax
from jax.sharding import PartitionSpec as P

HEAD_DIM = 64


def page_partial(query_rows, request_rows, page_rows, kv_cache, cache_len, page_table):
    count = query_rows.shape[0]
    width = query_rows.shape[1]
    local_heads = width // HEAD_DIM
    page_len = kv_cache.shape[2]
    slot_rows = page_table[request_rows, page_rows]
    lengths = cache_len[request_rows]
    keys = kv_cache[slot_rows, 0].reshape(count, page_len, local_heads, HEAD_DIM)
    values = kv_cache[slot_rows, 1].reshape(count, page_len, local_heads, HEAD_DIM)
    q_heads = query_rows.reshape(count, local_heads, HEAD_DIM)
    scores = jnp.einsum("nhe,nphe->nhp", q_heads, keys, preferred_element_type=jnp.float32)
    places = page_rows[:, None] * page_len + jnp.arange(page_len, dtype=jnp.int32)[None, :]
    valid = (places < lengths[:, None])[:, None, :]
    scores = jnp.where(valid, scores, -1e30)
    page_max = jnp.max(scores, axis=-1)
    weights = jnp.where(valid, jnp.exp(scores - page_max[..., None]), 0.0)
    page_sum = jnp.sum(weights, axis=-1)
    page_acc = jnp.einsum(
        "nhp,nphe->nhe", weights.astype(jnp.bfloat16), values, preferred_element_type=jnp.float32
    )
    return (page_max, page_sum, page_acc.reshape(count, width))


def body(tokens, norm_gain, w_qk, w_value, w_out, kv_cache, cache_len, page_table):
    gathered = lax.all_gather(tokens, "narrow", axis=1, tiled=True)
    floats = gathered.astype(jnp.float32)
    normed = (
        floats * lax.rsqrt(jnp.mean(floats * floats, axis=-1, keepdims=True) + 1e-06) * norm_gain
    ).astype(jnp.bfloat16)
    both = jnp.einsum("td,dcf->tcf", normed, w_qk, preferred_element_type=jnp.float32).astype(
        jnp.bfloat16
    )
    own_queries = both[:, 0, :]
    new_keys = both[:, 1, :]
    new_values = jnp.dot(normed, w_value, preferred_element_type=jnp.float32).astype(jnp.bfloat16)
    tok_count = tokens.shape[0]
    width = own_queries.shape[1]
    local_heads = width // HEAD_DIM
    page_count = page_table.shape[1]
    wide_count = lax.axis_size("wide")
    stride_len = wide_count // page_count
    my_index = lax.axis_index("wide")
    local_ids = jnp.arange(tok_count, dtype=jnp.int32)
    self_score = jnp.sum(
        own_queries.reshape(tok_count, local_heads, HEAD_DIM).astype(jnp.float32)
        * new_keys.reshape(tok_count, local_heads, HEAD_DIM).astype(jnp.float32),
        axis=-1,
    )
    value_heads = new_values.reshape(tok_count, local_heads, HEAD_DIM).astype(jnp.float32)
    all_queries = lax.all_gather(own_queries, "wide", axis=0, tiled=True)
    page_rows = jnp.repeat(jnp.arange(page_count, dtype=jnp.int32), tok_count)
    slot_local = jnp.tile(local_ids, page_count)
    page_offsets = (page_rows - page_rows % 2) * stride_len + page_rows % 2
    home_rows = (my_index - page_offsets) % wide_count
    request_rows = home_rows * tok_count + slot_local
    page_max, page_sum, page_acc = page_partial(
        all_queries[request_rows], request_rows, page_rows, kv_cache, cache_len, page_table
    )
    total = wide_count * tok_count
    max_table = jnp.full((total, local_heads), -1e30, jnp.float32).at[request_rows].set(page_max)
    best = lax.pmax(max_table, "wide")
    factor = jnp.exp(page_max - best[request_rows])
    scaled = (page_acc.reshape(-1, local_heads, HEAD_DIM) * factor[..., None]).reshape(-1, width)
    numer_table = jnp.zeros((total, width), jnp.float32).at[request_rows].set(scaled)
    denom_table = (
        jnp.zeros((total, local_heads), jnp.float32).at[request_rows].set(page_sum * factor)
    )
    numer, denom = (
        lax.psum_scatter(numer_table, "wide", scatter_dimension=0, tiled=True),
        lax.psum_scatter(denom_table, "wide", scatter_dimension=0, tiled=True),
    )
    best_home = lax.dynamic_slice_in_dim(best, my_index * tok_count, tok_count, 0)
    top = jnp.maximum(best_home, self_score)
    rescale = jnp.exp(best_home - top)
    self_factor = jnp.exp(self_score - top)
    numer = (
        numer.reshape(tok_count, local_heads, HEAD_DIM) * rescale[..., None]
        + self_factor[..., None] * value_heads
    )
    denom = denom * rescale + self_factor
    heads_out = (numer / denom[..., None]).reshape(tok_count, width).astype(jnp.bfloat16)
    partial_out = jnp.dot(heads_out, w_out, preferred_element_type=jnp.float32)
    return lax.psum_scatter(partial_out, "narrow", scatter_dimension=1, tiled=True).astype(
        jnp.bfloat16
    )


def solution(mesh):
    placed = (
        P("wide", "narrow"),
        P(),
        P(None, None, "narrow"),
        P(None, "narrow"),
        P("narrow", None),
        P("wide", None, None, "narrow"),
        P(),
        P(),
    )
    return jax.shard_map(
        body, mesh=mesh, in_specs=placed, out_specs=P("wide", "narrow"), check_vma=False
    )
```

profile of v0, /device:TPU:8, one launch (start us, length us, event | category | flops | bytes accessed | tf_op | source)
XLA Modules:
  0.0 1149.0 jit_solution(1433137674564910092)
XLA Ops:
  6.6 0.1 reshape.245
  6.6 0.1 tile.10
  6.7 12.5 %all_gather.6 = bf16[8,1024]{1,0:T(8,128)(2,1)S(1)} all-gather(bf16[8,256]{1,0:T(8,128)(2,1)} %param.8), channel_id=1, replica_groups=mesh['wide'=128,'narrow'=4] {'narrow'}, dimensions={1}, use_global_device_ids=true | all-gather | bytes 20480 | tf_op jit(solution)/shard_map/all_gather | solution.py:33
  19.3 0.1 fusion.20
  19.4 1.5 convolution_convert_fusion
  20.9 89.3 %all-gather = bf16[1024,1,256]{2,0,1:T(8,128)(2,1)S(1)} all-gather(bf16[8,1,256]{2,0,1:T(8,128)(2,1)S(1)} %slice.20), channel_id=2, replica_groups=mesh['wide'=128,'narrow'=4] {'wide'}, dimensions={0}, use_global_device_ids=true | all-gather | bytes 528384 | tf_op jit(solution)/shard_map/all_gather | solution.py:58
  110.3 0.7 gather_fusion.1
  111.0 0.1 reshape.323
  111.1 0.8 gather_fusion.2
  111.9 0.7 gather_fusion.3
  112.6 1.9 reshape.247
  114.5 2.8 fusion.2
  117.3 0.1 copy.27
  117.4 0.0 copy-done.1
  117.4 0.7 gather_fusion
  118.2 0.1 mul.110
  118.3 0.1 copy.21
  118.4 0.9 scatter_custom_fusion
  119.3 488.9 %pmax.7 = f32[1024,4]{1,0:T(8,128)S(1)} all-reduce(f32[1024,4]{1,0:T(8,128)S(1)} %scatter_custom_fusion), channel_id=1, replica_groups=mesh['wide'=128,'narrow'=4] {'wide'}, use_global_device_ids=true, to_apply=%region_3.4 | all-reduce | flops 4096 | bytes 32768 | tf_op jit(solution)/shard_map/pmax | solution.py:69
  608.3 0.6 gather_fusion.5
  608.9 0.1 copy.22
  608.9 0.1 copy.28
  609.1 0.7 gather_fusion.4
  609.8 1.9 reshape.248
  611.7 0.1 copy.23
  611.8 2.2 fusion
  614.0 0.1 broadcast_multiply_fusion
  614.2 0.1 reshape.304
  614.3 1.8 scatter_custom_fusion.1
  616.1 0.0 reduce-scatter.3.cloned.1.call-update
  616.2 0.0 reduce-scatter.5.cloned.1.call-start
  616.2 0.1 copy.24
  616.3 0.9 scatter_custom_fusion.2
  617.2 0.1 mul.120
  617.3 0.1 reduce_sum.28
  617.4 1.3 dynamic-slice
  619.3 491.0 %all-reduce.2 = f32[1024,4]{1,0:T(8,128)S(1)} all-reduce(f32[1024,4]{1,0:T(8,128)S(1)} %scatter_custom_fusion.2), channel_id=4, replica_groups=mesh['wide'=128,'narrow'=4] {'wide'}, use_global_device_ids=true, to_apply=%region_9.10.clone | all-reduce | flops 4096 | bytes 32768
  1110.2 0.7 fusion.28
  1110.9 0.1 div.15
  1111.0 0.1 div.16
  1111.1 0.1 mul.124
  1111.2 0.1 mul.125
  1111.2 0.1 mul.121
  1111.3 0.1 mul.122
  1111.4 2.3 fusion.9
  1113.7 0.0 reduce-scatter.5.cloned.1.call-update
  1113.8 27.1 %reduce-scatter.5.cloned.1.call-done = f32[8,256]{1,0:T(8,128)} async-done(((f32[8,1024]{1,0:T(8,128)}), f32[8,256]{1,0:T(8,128)}) %reduce-scatter.5.cloned.1.call-update) | async-done | bytes 8208 | tf_op jit(solution)/shard_map/reduce_scatter | solution.py:91
  1140.9 1.3 convert_element_type.50
  (24 shorter events, 0.2 us)
Async XLA Ops:
  6.5 105.4 %copy-start = (bf16[64,2,32,256]{3,2,1,0:T(8,128)(2,1)S(1)}, bf16[64,2,32,256]{3,2,1,0:T(8,128)(2,1)}, u32[]{:S(2)}) copy-start(bf16[64,2,32,256]{3,2,1,0:T(8,128)(2,1)} %param.13) | copy-start | bytes 6291460
  6.5 104.5 %copy-start.2 = (s32[1024,8]{0,1:T(8,128)S(1)}, s32[1024,8]{0,1:T(8,128)}, u32[]{:S(2)}) copy-start(s32[1024,8]{0,1:T(8,128)} %param.15) | copy-start | bytes 98308
  6.5 1104.9 %reduce-scatter.3.cloned.1.call-start = ((), (), s32[]{:S(2)}) async-start(), calls=%async_computation.2 | async-start | bytes 1056768 | tf_op jit(solution)/shard_map/reduce_scatter | solution.py:77
  114.5 2.9 copy-start.1
  608.3 0.8 copy-start.3
  614.2 497.2 %copy-start.4 = (f32[1024]{0:T(1024)S(1)}, f32[1024]{0:T(1024)}, u32[]{:S(2)}) copy-start(f32[1024]{0:T(1024)} %param.9) | copy-start | bytes 12292
  616.2 524.7 %reduce-scatter.5.cloned.1.call-start = ((), (), s32[]{:S(2)}) async-start(), calls=%async_computation.3 | async-start | bytes 40960 | tf_op jit(solution)/shard_map/reduce_scatter | solution.py:91
Sparse Core Ops, SparseCore 0:
  616.3 258.9 reduce-scatter.2
  1113.9 26.9 reduce-scatter.4
where the time goes:
time: 1150 us
  blocking collectives  1080 us (94%)
  waiting for transfers between devices  27.2 us (2%)
  local copies, waits for them, and re-layouts  14.5 us (1%)
  between operations  14.2 us (1%)
    unnamed x1, blocking collectives  491 us
    pmax x1, blocking collectives, body(): best = lax.pmax(max_table, 'wide')  489 us
    all_gather x1, blocking collectives, body(): all_queries = lax.all_gather(own_queries, 'wide', axis=0, tiled=True)  89.3 us
    reduce_scatter x1, waiting for transfers between devices, body(): lax.psum_scatter(partial_out, 'narrow', scatter_dimension=1, tiled=True)  27.1 us
  transfers between devices with their start and end apart: 2, of which 1 were waited for; matrix products, arithmetic and copies ran while one was open for 0% of the time, Pallas kernels for 0%

commit v1 on v0

--- a/solution.py
+++ b/solution.py
@@ -55,7 +55,9 @@
         axis=-1,
     )
     value_heads = new_values.reshape(tok_count, local_heads, HEAD_DIM).astype(jnp.float32)
-    all_queries = lax.all_gather(own_queries, "wide", axis=0, tiled=True)
+    all_queries = jnp.concatenate(
+        lax.all_to_all(jnp.stack([own_queries] * lax.axis_size("wide")), "wide", 0, 0), axis=0
+    )
     page_rows = jnp.repeat(jnp.arange(page_count, dtype=jnp.int32), tok_count)
     slot_local = jnp.tile(local_ids, page_count)
     page_offsets = (page_rows - page_rows % 2) * stride_len + page_rows % 2

time: 1150 us -> 1100 us (0.957)
  blocking collectives: 1080 us -> 990 us
  waiting for transfers between devices: 27.2 us -> 51.1 us
  starting transfers between devices: 0.04 us -> 20.1 us
    all_gather x1 -> x0, blocking collectives: 89.3 us -> none  [body(): all_queries = lax.all_gather(own_queries, 'wide', axis=0, tiled=True)]
    all_to_all x0 -> x1, waiting for transfers between devices: none -> 23.9 us  [body(): lax.all_to_all(jnp.stack([own_queries] * lax.axis_size('wide')), 'wide',...]
    all_to_all x0 -> x1, starting transfers between devices: none -> 20 us  [body(): lax.all_to_all(jnp.stack([own_queries] * lax.axis_size('wide')), 'wide',...]
  transfers between devices with their start and end apart: 2 -> 3, of which waited for: 1 -> 2; matrix products, arithmetic and copies ran while one was open for 0% -> 1% of each run, Pallas kernels for 0% -> 0%
where the time goes in v1:
time: 1100 us
  blocking collectives  990 us (90%)
  waiting for transfers between devices  51.1 us (5%)
  starting transfers between devices  20.1 us (2%)
  local copies, waits for them, and re-layouts  16.4 us (1%)
  between operations  14.2 us (1%)
    unnamed x1, blocking collectives  492 us
    pmax x1, blocking collectives, body(): best = lax.pmax(max_table, 'wide')  486 us
    reduce_scatter x1, waiting for transfers between devices, body(): lax.psum_scatter(partial_out, 'narrow', scatter_dimension=1, tiled=True)  27.2 us
    all_to_all x1, waiting for transfers between devices, body(): lax.all_to_all(jnp.stack([own_queries] * lax.axis_size('wide')), 'wide',...  23.9 us
  transfers between devices with their start and end apart: 3, of which 2 were waited for; matrix products, arithmetic and copies ran while one was open for 1% of the time, Pallas kernels for 0%

profile of v1, /device:TPU:8, one launch (start us, length us, event | category | flops | bytes accessed | tf_op | source)
XLA Modules:
  0.0 1103.3 jit_solution(1511308425497121254)
XLA Ops:
  6.5 12.5 %all_gather.3 = bf16[8,1024]{1,0:T(8,128)(2,1)S(1)} all-gather(bf16[8,256]{1,0:T(8,128)(2,1)} %param.8), channel_id=1, replica_groups=mesh['wide'=128,'narrow'=4] {'narrow'}, dimensions={1}, use_global_device_ids=true | all-gather | bytes 20480 | tf_op jit(solution)/shard_map/all_gather | solution.py:33
  19.1 0.1 fusion.20
  19.2 1.5 convolution_convert_fusion
  20.7 0.9 stack.3
  21.6 20.0 %all-to-all-start = ((bf16[128,8,256]{2,1,0:T(8,128)(2,1)}), bf16[128,8,256]{2,1,0:T(8,128)(2,1)}, u32[]{:S(2)}, u32[]{:S(2)}) async-start(bf16[128,8,256]{2,1,0:T(8,128)(2,1)} %stack.3), calls=%async_computation | async-start | bytes 1048576 | tf_op jit(solution)/shard_map/all_to_all | solution.py:59
  41.6 0.0 reduce-scatter.3.cloned.1.call-start
  41.6 0.1 reshape.250
  41.7 0.1 tile.10
  41.9 0.8 gather_fusion.2
  42.7 0.7 gather_fusion.3
  43.4 1.9 reshape.253
  45.3 0.1 mul.110
  45.4 0.7 gather_fusion.4
  46.1 1.8 reshape.254
  48.0 0.7 gather_fusion
  48.7 23.9 %all-to-all-done = bf16[128,8,256]{2,1,0:T(8,128)(2,1)} async-done(((bf16[128,8,256]{2,1,0:T(8,128)(2,1)}), bf16[128,8,256]{2,1,0:T(8,128)(2,1)}, u32[]{:S(2)}, u32[]{:S(2)}) %all-to-all-start) | async-done | bytes 524320 | tf_op jit(solution)/shard_map/all_to_all | solution.py:59
  72.6 1.8 gather_fusion.1
  74.3 0.1 reshape.328
  74.4 2.8 fusion.2
  77.2 0.1 copy.27
  77.4 0.1 copy.21
  77.5 0.9 scatter_custom_fusion
  78.3 486.0 %pmax.7 = f32[1024,4]{1,0:T(8,128)S(1)} all-reduce(f32[1024,4]{1,0:T(8,128)S(1)} %scatter_custom_fusion), channel_id=1, replica_groups=mesh['wide'=128,'narrow'=4] {'wide'}, use_global_device_ids=true, to_apply=%region_3.4 | all-reduce | flops 4096 | bytes 32768 | tf_op jit(solution)/shard_map/pmax | solution.py:71
  564.4 0.6 gather_fusion.5
  565.0 0.1 copy.22
  565.0 0.1 copy.28
  565.2 0.1 copy.23
  565.3 2.2 fusion
  567.5 0.1 broadcast_multiply_fusion
  567.7 0.1 reshape.310
  567.8 1.8 scatter_custom_fusion.1
  569.7 0.0 reduce-scatter.5.cloned.1.call-start
  569.7 0.1 mul.120
  569.8 0.1 reduce_sum.28
  569.9 1.3 dynamic-slice
  571.8 0.1 copy.24
  571.9 0.9 scatter_custom_fusion.2
  572.8 491.6 %all-reduce.2 = f32[1024,4]{1,0:T(8,128)} all-reduce(f32[1024,4]{1,0:T(8,128)S(1)} %scatter_custom_fusion.2), channel_id=3, replica_groups=mesh['wide'=128,'narrow'=4] {'wide'}, use_global_device_ids=true, to_apply=%region_9.10.clone | all-reduce | flops 4096 | bytes 32768
  1064.4 0.7 fusion.28
  1065.1 0.1 div.15
  1065.1 0.1 div.16
  1065.2 0.1 mul.124
  1065.3 0.1 mul.125
  1065.4 0.1 mul.121
  1065.5 0.1 mul.122
  1065.5 2.3 fusion.9
  1067.9 27.2 %reduce-scatter.5.cloned.1.call-done = f32[8,256]{1,0:T(8,128)} async-done(((f32[8,1024]{1,0:T(8,128)}), f32[8,256]{1,0:T(8,128)}) %reduce-scatter.5.cloned.1.call-update) | async-done | bytes 8208 | tf_op jit(solution)/shard_map/reduce_scatter | solution.py:93
  1095.1 1.3 convert_element_type.50
  (24 shorter events, 0.2 us)
Async XLA Ops:
  6.5 36.1 %copy-start = (bf16[64,2,32,256]{3,2,1,0:T(8,128)(2,1)S(1)}, bf16[64,2,32,256]{3,2,1,0:T(8,128)(2,1)}, u32[]{:S(2)}) copy-start(bf16[64,2,32,256]{3,2,1,0:T(8,128)(2,1)} %param.13) | copy-start | bytes 6291460
  6.5 35.3 %copy-start.2 = (s32[1024,8]{0,1:T(8,128)S(1)}, s32[1024,8]{0,1:T(8,128)}, u32[]{:S(2)}) copy-start(s32[1024,8]{0,1:T(8,128)} %param.15) | copy-start | bytes 98308
  21.6 50.9 %all-to-all-start = ((bf16[128,8,256]{2,1,0:T(8,128)(2,1)}), bf16[128,8,256]{2,1,0:T(8,128)(2,1)}, u32[]{:S(2)}, u32[]{:S(2)}) async-start(bf16[128,8,256]{2,1,0:T(8,128)(2,1)} %stack.3), calls=%async_computation | async-start | bytes 1048576 | tf_op jit(solution)/shard_map/all_to_all | solution.py:59
  41.6 1024.0 %reduce-scatter.3.cloned.1.call-start = ((), (), s32[]{:S(2)}) async-start(), calls=%async_computation.3 | async-start | bytes 1056768 | tf_op jit(solution)/shard_map/reduce_scatter | solution.py:79
  46.1 1.9 copy-start.1
  567.7 497.9 %copy-start.3 = (f32[1024]{0:T(1024)S(1)}, f32[1024]{0:T(1024)}, u32[]{:S(2)}) copy-start(f32[1024]{0:T(1024)} %param.9) | copy-start | bytes 12292
  569.7 525.5 %reduce-scatter.5.cloned.1.call-start = ((), (), s32[]{:S(2)}) async-start(), calls=%async_computation.4 | async-start | bytes 40960 | tf_op jit(solution)/shard_map/reduce_scatter | solution.py:93
Sparse Core Ops, SparseCore 0:
  569.8 259.0 reduce-scatter.2
  1068.0 27.0 reduce-scatter.4
